TPU v7x, 32 devices: a whole 2x2x4 slice. The times are simulated.
32 devices in a mesh: rows: 8 (over y, x, core), rhs: 4 (over z).
Axes of the slice: x: 2, y: 2, z: 4, core: 2. Of those that a mesh axis runs over, the one named last changes fastest.
Arguments:
- samples: float32 [65536, 16], P(('rows', 'rhs')), may hold values from -5 to 5
- freq_table: float32 [4096, 16], replicated, may hold values from -3 to 3
- feature_seeds: int32 [512], replicated, may hold values from 0 to 4095
- phases: float32 [512], replicated, may hold values from -3.140625 to 3.140625
- treatment_features: bfloat16 [65536, 512], P('rows', 'rhs'), may hold values from -2.5 to 2.5, as said below
Outputs:
- coefficients: float32 [512, 512], replicated
- fitted: float32 [65536, 512], P(('rows', 'rhs'))
Inputs may be any that keep to these rules, and one draw needn't show every extreme that they name: `treatment_features`: treatment features depend on the instrument values.
All inputs are finite; a program needn't handle non-finite values.
Results may differ from a plain program's by a relative error of at most 0.0008.
The roundings to bfloat16 on the way count: a program that leaves them out, or rounds other values in their place, can miss the bound.
Values may be sent and summed in bfloat16 or wider, within the bound.
A program may use at most 64 MiB of HBM per device.

v0:
```python
import functools
import math

import jax
import jax.numpy as jnp
from jax import lax
from jax.experimental import pallas as pl
from jax.experimental.pallas import tpu as pltpu
from jax.sharding import PartitionSpec as P

ridge = 0.05
MESH = pl.DeviceIdType.MESH
HIGHEST = lax.Precision.HIGHEST
VMEM = pl.BlockSpec(memory_space=pltpu.VMEM)
NT = (((1,), (1,)), ((), ()))
TILE = 128
SIN_TERMS = [3.1415926532437486, -5.167712741221454, 2.5501627947182053, -0.5992474048759052, 0.08203123002136099, -0.00700050017770637]


def split_low(x):
    high = lax.reduce_precision(x, 8, 7)
    rest = x - high
    middle = lax.reduce_precision(rest, 8, 7)
    low = rest - middle
    return tuple(t.astype(jnp.bfloat16) for t in (high, middle, low))


def feature_kernel(group, parts, x_ref, f_ref, t_hbm, gram_ref, cross_ref, own_ref, xs, t_ref, rhs, acc, *rest):
    phis, (send, recv, local) = rest[:parts], rest[parts:]
    me = lax.axis_index("rhs")
    own, panel = x_ref.shape[1], t_ref.shape[1]
    chunk = own // parts
    load = pltpu.make_async_copy(t_hbm, t_ref, local)
    load.start()
    barrier = pltpu.get_barrier_semaphore()
    for d in range(1, group):
        pl.semaphore_signal(
            barrier, inc=1, device_id={"rhs": lax.rem(me + d, group)}, device_id_type=MESH
        )
    pl.semaphore_wait(barrier, group - 1)

    def moving(d, way):
        block = me - way * (d - 1)
        return pltpu.make_async_remote_copy(
            src_ref=x_ref if isinstance(d, int) and d == 1 else xs.at[block],
            dst_ref=xs.at[block],
            send_sem=send.at[(way + 1) // 2, d],
            recv_sem=recv.at[(way + 1) // 2, d],
            device_id={"rhs": me + way},
            device_id_type=MESH,
        )

    def arriving(d, way):
        block = me - way * d
        return pltpu.make_async_remote_copy(
            src_ref=xs.at[block],
            dst_ref=xs.at[block],
            send_sem=send.at[(way + 1) // 2, d],
            recv_sem=recv.at[(way + 1) // 2, d],
            device_id={"rhs": me - way},
            device_id_type=MESH,
        )

    def inside(v):
        return jnp.logical_and(v >= 0, v < group)

    def pass_on(d, way):
        pl.when(jnp.logical_and(inside(me + way), inside(me - way * (d - 1))))(
            lambda: moving(d, way).start()
        )

    xs[me] = x_ref[...]
    for way in (1, -1):
        pass_on(1, way)
    acc[...] = jnp.zeros_like(acc)
    load.wait()
    near = jnp.minimum(me, group - 1 - me)
    scale = math.sqrt(2.0 * math.sqrt(2.0))

    @pl.loop(0, group)
    def _(d):
        for way in (1, -1):

            @pl.when(jnp.logical_and(d > 0, inside(me - way * d)))
            def _():
                arriving(d, way).wait_recv()

            pl.when(jnp.logical_and(d > 0, d + 1 < group))(lambda: pass_on(d + 1, way))

        step = (d + 1) // 2
        both = jnp.where(d % 2 == 1, me - step, me + step)
        single = jnp.where(me < group - 1 - me, me + d - near, me - d + near)
        block = jnp.where(d <= 2 * near, both, single)
        for part in range(parts):
            x = xs[block, :, part * chunk : (part + 1) * chunk]
            high = x.astype(jnp.bfloat16)
            left = x - high.astype(jnp.float32)
            middle = left.astype(jnp.bfloat16)
            low = (left - middle.astype(jnp.float32)).astype(jnp.bfloat16)
            ones = jnp.ones(x.shape, jnp.bfloat16)
            rows = jnp.concatenate([high, high, middle, middle, high, low, ones], axis=0)
            turns = jnp.dot(f_ref[...], rows, preferred_element_type=jnp.float32)
            r = turns - jnp.round(turns)
            u = r * r
            s = jnp.full_like(u, SIN_TERMS[-1] * scale)
            for term in reversed(SIN_TERMS[:-1]):
                s = s * u + term * scale
            s = s * r
            phis[part][...] = (math.sqrt(2.0) - s * s).astype(jnp.bfloat16)
            mine = phis[part][pl.ds(pl.multiple_of(me * panel, panel), panel), :]
            rhs[part, :, :panel] = mine.T
            here = pl.multiple_of(block * own + part * chunk, chunk)
            rhs[part, :, panel:] = t_ref[pl.ds(here, chunk), :]
            acc[...] += jnp.dot(phis[part][...], rhs[part], preferred_element_type=jnp.float32)

        @pl.when(d == 0)
        def _():
            for part in range(parts):
                own_ref[part] = phis[part][...]

    for d in range(1, group):
        for way in (1, -1):
            pl.when(jnp.logical_and(inside(me + way), inside(me - way * (d - 1))))(
                lambda: moving(d, way).wait_send()
            )
    gram_ref[...] = acc[:, :panel]
    cross_ref[...] = acc[:, panel:]


def panels(x, freqs, targets):
    group = lax.axis_size("rhs")
    depth, own = x.shape
    features = freqs.shape[0]
    panel = targets.shape[1]
    chunk = min(own, 512)
    parts = own // chunk
    sems = pltpu.SemaphoreType.DMA
    return pl.pallas_call(
        functools.partial(feature_kernel, group, parts),
        in_specs=[VMEM, VMEM, pl.BlockSpec(memory_space=pl.ANY)],
        out_specs=[VMEM] * 3,
        out_shape=[
            jax.ShapeDtypeStruct((features, panel), jnp.float32),
            jax.ShapeDtypeStruct((features, panel), jnp.float32),
            jax.ShapeDtypeStruct((parts, features, chunk), jnp.bfloat16),
        ],
        scratch_shapes=[
            pltpu.VMEM((group, depth, own), jnp.float32),
            pltpu.VMEM(targets.shape, targets.dtype),
            pltpu.VMEM((parts, chunk, 2 * panel), jnp.bfloat16),
            pltpu.VMEM((features, 2 * panel), jnp.float32),
        ]
        + [pltpu.VMEM((features, chunk), jnp.bfloat16)] * parts
        + [sems((2, group)), sems((2, group)), sems(())],
        compiler_params=pltpu.CompilerParams(collective_id=0, has_side_effects=True),
    )(x, freqs, targets)


def exchange(R, Z, w_ref, got, out, sems):
    send, recv, zsend, zrecv, psend, precv, csend, crecv = sems
    r, z = lax.axis_index("rows"), lax.axis_index("rhs")
    core, spot, half = lax.rem(r, 2), r // 2, R // 2

    def copy(src, dst, out_sem, in_sem, d, peer):
        return pltpu.make_async_remote_copy(
            src_ref=src,
            dst_ref=dst,
            send_sem=out_sem.at[d],
            recv_sem=in_sem.at[d],
            device_id=peer,
            device_id_type=MESH,
        )

    def scatter(d):
        peer = lax.rem(r + d, R)
        return copy(w_ref.at[peer], got.at[d], send, recv, d, {"rows": peer})

    def along(d):
        mine = out.at[r, z]
        return copy(mine, mine, zsend, zrecv, d, {"rhs": lax.rem(z + d, Z)})

    def across(d):
        peer = lax.rem(spot + d, half) * 2 + core
        return copy(out.at[r], out.at[r], psend, precv, d, {"rows": peer})

    def aside(d):
        where = out.at[lax.rem(spot - d + half, half) * 2 + core]
        return copy(where, where, csend, crecv, d, {"rows": r + 1 - 2 * core})

    def first():
        for d in range(1, R):
            scatter(d).start()

    def second():
        total = w_ref[r]
        for d in range(1, R):
            scatter(d).wait()
            total = total + got[d]
        out[r, z] = total
        for d in range(1, Z):
            along(d).start()

    def third():
        for d in range(1, Z):
            along(d).wait()
        for d in range(1, half):
            across(d).start()
        aside(0).start()

    def fourth():
        for d in range(1, half):
            across(d).wait()
            aside(d).start()

    def last():
        for d in range(half):
            aside(d).wait()

    return first, second, third, fourth, last


def invert_two(a, b, d):
    scale = 1.0 / (a * d - b * b)
    return d * scale, -b * scale, a * scale


def invert_four(p):
    e0, e1, e2 = invert_two(p[0][0], p[0][1], p[1][1])
    y00 = e0 * p[0][2] + e1 * p[1][2]
    y01 = e0 * p[0][3] + e1 * p[1][3]
    y10 = e1 * p[0][2] + e2 * p[1][2]
    y11 = e1 * p[0][3] + e2 * p[1][3]
    s0 = p[2][2] - (p[0][2] * y00 + p[1][2] * y10)
    s1 = p[2][3] - (p[0][2] * y01 + p[1][2] * y11)
    s2 = p[3][3] - (p[0][3] * y01 + p[1][3] * y11)
    t0, t1, t2 = invert_two(s0, s1, s2)
    q02 = -(y00 * t0 + y01 * t1)
    q03 = -(y00 * t1 + y01 * t2)
    q12 = -(y10 * t0 + y11 * t1)
    q13 = -(y10 * t1 + y11 * t2)
    q00 = e0 - (q02 * y00 + q03 * y01)
    q01 = e1 - (q02 * y10 + q03 * y11)
    q11 = e2 - (q12 * y10 + q13 * y11)
    return [
        [q00, q01, q02, q03],
        [q01, q11, q12, q13],
        [q02, q12, t0, t1],
        [q03, q13, t1, t2],
    ]


def invert_block(ref, dst):
    q = 4
    groups = TILE // 8
    a = [ref[8 * i : 8 * i + 8, :] for i in range(groups)]
    lane = lax.broadcasted_iota(jnp.int32, (8, TILE), 1)
    sub = lax.broadcasted_iota(jnp.int32, (8, TILE), 0)
    lane1 = lane[:1]
    for k in range(0, TILE, q):
        g, o = k // 8, k % 8
        c = [
            [jnp.broadcast_to(v[:, k + j : k + j + 1], (8, TILE)) for j in range(q)]
            for v in a
        ]
        if k == 0:
            p = [[c[g][j][o + i : o + i + 1, :] for j in range(q)] for i in range(q)]
        inv = invert_four(p)
        n = k + q
        if n < TILE:
            after = [jnp.broadcast_to(a[g][:, n + j : n + j + 1], (8, TILE)) for j in range(q)]
            mine = [[v[o + i : o + i + 1, :] for v in after] for i in range(q)]
            if n // 8 != g:
                after = [
                    jnp.broadcast_to(a[n // 8][:, n + j : n + j + 1], (8, TILE)) for j in range(q)
                ]
            below = [[v[n % 8 + i : n % 8 + i + 1, :] for v in after] for i in range(q)]
            t = [[sum(inv[i][b] * mine[b][j] for b in range(q)) for j in range(q)] for i in range(q)]
            p = [
                [
                    below[i][j] - sum(mine[b][i] * t[b][j] for b in range(q)) if j >= i else None
                    for j in range(q)
                ]
                for i in range(q)
            ]
        inside = jnp.logical_and(lane >= k, lane < k + q)
        pivot = [
            jnp.where(lane1 == k + i, 1.0, jnp.where(inside[:1], 0.0, a[g][o + i : o + i + 1, :]))
            for i in range(q)
        ]
        w = [sum(inv[i][j] * pivot[j] for j in range(q)) for i in range(q)]
        wb = [jnp.broadcast_to(v, (8, TILE)) for v in w]
        new = []
        for i in range(groups):
            v = jnp.where(inside, 0.0, a[i])
            v = v - ((c[i][0] * wb[0] + c[i][1] * wb[1]) + (c[i][2] * wb[2] + c[i][3] * wb[3]))
            if i == g:
                for j in range(q):
                    v = jnp.where(sub == o + j, wb[j], v)
            new.append(v)
        a = new
    for i in range(groups):
        dst[8 * i : 8 * i + 8, :] = a[i]


def solve_kernel(R, Z, count, w_ref, v_ref, coef_ref, low_ref, gram, right, lower, inverse, got, out, vgot, vout, *sems):
    rows, panel = w_ref.shape[1:]
    size = gram.shape[0]
    r, z = lax.axis_index("rows"), lax.axis_index("rhs")
    barrier = pltpu.get_barrier_semaphore()
    for d in range(1, R):
        pl.semaphore_signal(
            barrier, inc=1, device_id={"rows": lax.rem(r + d, R)}, device_id_type=MESH
        )
    for d in range(1, Z):
        pl.semaphore_signal(
            barrier, inc=1, device_id={"rhs": lax.rem(z + d, Z)}, device_id_type=MESH
        )
    pl.semaphore_wait(barrier, R + Z - 2)
    for stage in exchange(R, Z, w_ref, got, out, sems[:8]):
        stage()
    stages = exchange(R, Z, v_ref, vgot, vout, sems[8:])
    stages[0]()

    def spread(source, dest):
        for i in range(R):
            for j in range(Z):
                dest[i * rows : (i + 1) * rows, j * panel : (j + 1) * panel] = source[
                    i, j
                ] * (1.0 / count)

    spread(out, gram)
    row = lax.broadcasted_iota(jnp.int32, (TILE, TILE), 0)
    col = lax.broadcasted_iota(jnp.int32, (TILE, TILE), 1)
    eye = jnp.where(row == col, jnp.float32(ridge), 0.0)
    blocks = size // TILE
    dot = functools.partial(jnp.dot, precision=HIGHEST, preferred_element_type=jnp.float32)

    def at(i):
        return slice(i * TILE, (i + 1) * TILE)

    for k in range(blocks):
        gram[at(k), at(k)] += eye

    @pl.loop(0, blocks)
    def _(k):
        mine = pl.ds(pl.multiple_of(k * TILE, TILE), TILE)
        inverse[blocks] = gram[mine, mine]
        invert_block(inverse.at[blocks], inverse.at[k])
        gram_row = dot(inverse[k], gram[mine, :])

        @pl.loop(k + 1, blocks)
        def _(i):
            below = pl.ds(pl.multiple_of(i * TILE, TILE), TILE)
            left = gram[below, mine]
            lower[below, mine] = left
            gram[below, :] -= dot(left, gram_row)

        gram[mine, :] = gram_row
        for i, stage in enumerate(stages[1:]):
            pl.when(k == min(i, blocks - 1))(stage)

    spread(vout, right)
    for k in range(blocks):
        value = dot(inverse[k], right[at(k), :])
        right[at(k), :] = value
        if k + 1 < blocks:
            tail = slice((k + 1) * TILE, size)
            right[tail, :] -= dot(lower[tail, at(k)], value)
    for k in reversed(range(blocks)):
        value = right[at(k), :]
        coef_ref[at(k), :] = value
        low_ref[at(k), :] = value.astype(jnp.bfloat16)
        if k:
            right[: k * TILE, :] -= dot(gram[: k * TILE, at(k)], value)


def solve(count, w, v):
    R, Z = lax.axis_size("rows"), lax.axis_size("rhs")
    size, panel = w.shape
    rows, columns = size // R, Z * panel
    split = (R, rows, panel)
    sems = pltpu.SemaphoreType.DMA
    blocks = size // TILE
    big = pltpu.VMEM((R, Z, rows, panel), jnp.float32)
    return pl.pallas_call(
        functools.partial(solve_kernel, R, Z, count),
        out_shape=[
            jax.ShapeDtypeStruct((size, columns), jnp.float32),
            jax.ShapeDtypeStruct((size, columns), jnp.bfloat16),
        ],
        in_specs=[VMEM, VMEM],
        out_specs=[VMEM, VMEM],
        scratch_shapes=[
            pltpu.VMEM((size, size), jnp.float32),
            pltpu.VMEM((size, columns), jnp.float32),
            pltpu.VMEM((size, size), jnp.float32),
            pltpu.VMEM((blocks + 1, TILE, TILE), jnp.float32),
            pltpu.VMEM(split, jnp.float32),
            big,
            pltpu.VMEM(split, jnp.float32),
            big,
        ]
        + ([sems((R,))] * 2 + [sems((Z,))] * 2 + [sems((R,))] * 4) * 2,
        compiler_params=pltpu.CompilerParams(collective_id=1, has_side_effects=True),
    )(w.reshape(split), v.reshape(split))


def body(samples, freq_table, feature_seeds, phases, treatment_features):
    count = samples.shape[0] * lax.axis_size("rows") * lax.axis_size("rhs")
    turn = jnp.float32(1.0 / (2.0 * math.pi))
    high, middle, low = split_low(freq_table[feature_seeds] * turn)
    shift = jnp.stack(split_low(phases * turn), axis=1)
    shift = jnp.pad(shift, ((0, 0), (0, high.shape[1] - shift.shape[1])))
    freqs = jnp.concatenate([high, middle, high, middle, low, high, shift], axis=1)
    w, v, own = panels(samples.T, freqs, treatment_features)
    coefficients, low_coef = solve(count, w, v)
    fitted = lax.dot_general(
        own, low_coef, (((1,), (0,)), ((), ())), preferred_element_type=jnp.float32
    ).reshape(samples.shape[0], low_coef.shape[1])
    return (coefficients, fitted)


def solution(mesh):
    placed = (P(("rows", "rhs"), None), P(), P(), P(), P("rows", "rhs"))
    return jax.shard_map(
        body, mesh=mesh, in_specs=placed, out_specs=(P(), P(("rows", "rhs"), None)), check_vma=False
    )
```

profile of v0, /device:TPU:0, one launch (start us, length us, event | category | flops | bytes accessed | tf_op | source)
XLA Modules:
  0.0 88.5 jit_solution(7166289175293367048)
XLA Ops:
  0.6 0.7 compare_select_fusion
  1.3 0.7 reduce-precision_convert_fusion.3
  2.1 0.2 copy.19
  2.3 1.5 %copy.17 = f32[4096,16]{1,0:T(8,128)S(1)} copy(f32[4096,16]{0,1:T(8,128)} %param.6) | data formatting | bytes 524288 | tf_op args[1]
  3.8 1.0 %gather_fusion = f32[512,16]{1,0:T(8,128)S(1)} fusion(f32[4096,16]{1,0:T(8,128)S(1)} %copy.17, s32[1024]{0:T(1024)S(1)} %pad_clamp_fusion), kind=kCustom, calls=%fused_computation | custom fusion | bytes 67584 | tf_op jit(solution)/shard_map/gather | solution.py:411
  4.9 0.1 fusion.2
  5.0 1.0 %concatenate.3.f_ref = bf16[512,112]{1,0:T(8,128)(2,1)} concatenate(bf16[512,16]{1,0:T(8,128)(2,1)S(1)} %get-tuple-element.14, bf16[512,16]{1,0:T(8,128)(2,1)S(1)} %get-tuple-element.13, bf16[512,16]{1,0:T(8,128)(2,1)S(1)} %get-tuple-element.14, bf16[512,16]{1,0:T(8,128)(2,1)S(1)} %get-tuple-element.13, bf16[512,16]{1,0:T(8,128)(2,1)S(1)} %get-tuple-element.12, ...), dimensions={1} | concatenate | bytes 229376 | tf_op jit(solution)/shard_map/concatenate | solution.py:414
  6.0 22.5 %shard_map.68 = (f32[512,128]{1,0:T(8,128)}, f32[512,128]{1,0:T(8,128)}, bf16[4,512,512]{2,1,0:T(8,128)(2,1)}) custom-call(f32[16,2048]{1,0:T(8,128)} %bitcast.11, bf16[512,112]{1,0:T(8,128)(2,1)} %concatenate.3.f_ref, bf16[8192,128]{1,0:T(8,128)(2,1)} %t_hbm.1), custom_call_target="tpu_custom_call" | custom-call | tf_op jit(solution)/shard_map/pallas_call | solution.py:138
  28.5 53.9 %shard_map.69 = (f32[512,512]{1,0:T(8,128)}, bf16[512,512]{1,0:T(8,128)(2,1)}) custom-call(f32[8,64,128]{2,1,0:T(8,128)} %bitcast.9, f32[8,64,128]{2,1,0:T(8,128)} %bitcast.10), custom_call_target="tpu_custom_call" | custom-call | tf_op jit(solution)/shard_map/pallas_call | solution.py:385
  82.4 0.0 copy-start
  82.4 5.1 %fusion = f32[4,512,512]{2,1,0:T(8,128)} fusion(bf16[4,512,512]{2,1,0:T(8,128)(2,1)} %get-tuple-element.10, bf16[512,512]{1,0:T(8,128)(2,1)} %get-tuple-element.11), kind=kOutput, calls=%fused_computation.1 | convolution fusion | flops 1073741824 | bytes 6815744 | tf_op jit(solution)/shard_map/dot_general | solution.py:417
  87.5 0.0 copy-done
  87.5 1.0 %copy.23 = f32[512,512]{1,0:T(8,128)} copy(f32[512,512]{1,0:T(8,128)S(1)} %copy-done) | data formatting | bytes 2097152
  (6 shorter events, 0.1 us)
Async XLA Ops:
  82.4 5.1 %copy-start = (f32[512,512]{1,0:T(8,128)S(1)}, f32[512,512]{1,0:T(8,128)}, u32[]{:S(2)}) copy-start(f32[512,512]{1,0:T(8,128)} %get-tuple-element.20) | copy-start | bytes 3145732
where the time goes:
time: 88.7 us; the launch traced here: 88.5 us
  Pallas kernels  76.4 us (86%)
  matrix products  5.06 us (6%)
  local copies, waits for them, and re-layouts  4.78 us (5%)
  other arithmetic  1.47 us (2%)
    pallas_call x1, Pallas kernels, solve(): pl.pallas_call(functools.partial(solve_kernel, R, Z, count), out_shape=[j...  53.9 us
    pallas_call x1, Pallas kernels, panels(): pl.pallas_call(functools.partial(feature_kernel, group, parts), in_specs=...  22.5 us
    dot_general x1, matrix products, body(): lax.dot_general(own, low_coef, (((1,), (0,)), ((), ())), preferred_elemen...  5.06 us
    unnamed x4, local copies, waits for them, and re-layouts  2.52 us

commit v1 on v0

v1 whole, which is shorter than its diff:
```python
import functools
import math

import jax
import jax.numpy as jnp
from jax import lax
from jax.experimental import pallas as pl
from jax.experimental.pallas import tpu as pltpu
from jax.sharding import PartitionSpec as P

ridge = 0.05
MESH = pl.DeviceIdType.MESH
HIGHEST = lax.Precision.HIGHEST
VMEM = pl.BlockSpec(memory_space=pltpu.VMEM)
ANY = pl.BlockSpec(memory_space=pl.ANY)
TILE = 128
SIN_TERMS = [3.141592580044735, -5.1677068789267455, 2.550031377285281, -0.598045174146624, 0.07722012899537994]


def split_low(x):
    high = lax.reduce_precision(x, 8, 7)
    rest = x - high
    middle = lax.reduce_precision(rest, 8, 7)
    low = rest - middle
    return tuple(t.astype(jnp.bfloat16) for t in (high, middle, low))


def features(x, f):
    high = x.astype(jnp.bfloat16)
    left = x - high.astype(jnp.float32)
    middle = left.astype(jnp.bfloat16)
    low = (left - middle.astype(jnp.float32)).astype(jnp.bfloat16)
    ones = jnp.ones(x.shape, jnp.bfloat16)
    rows = jnp.concatenate([high, high, middle, middle, high, low, ones], axis=0)
    turns = jnp.dot(f, rows, preferred_element_type=jnp.float32)
    r = turns - jnp.round(turns)
    u = r * r
    scale = math.sqrt(2.0 * math.sqrt(2.0))
    s = u * (SIN_TERMS[-1] * scale) + SIN_TERMS[-2] * scale
    for term in reversed(SIN_TERMS[:-2]):
        s = s * u + term * scale
    s = s * r
    return (math.sqrt(2.0) - s * s).astype(jnp.bfloat16)


def exchange(R, Z, count, w_ref, got, out, sems):
    send, recv, zsend, zrecv, psend, precv, csend, crecv = sems
    r, z = lax.axis_index("rows"), lax.axis_index("rhs")
    core, spot, half = lax.rem(r, 2), r // 2, R // 2

    def copy(src, dst, out_sem, in_sem, d, peer):
        return pltpu.make_async_remote_copy(
            src_ref=src,
            dst_ref=dst,
            send_sem=out_sem.at[d],
            recv_sem=in_sem.at[d],
            device_id=peer,
            device_id_type=MESH,
        )

    def scatter(d):
        peer = lax.rem(r + d, R)
        return copy(w_ref.at[peer], got.at[d], send, recv, d, {"rows": peer})

    def along(d):
        mine = out.at[r, z]
        return copy(mine, mine, zsend, zrecv, d, {"rhs": lax.rem(z + d, Z)})

    def across(d):
        peer = lax.rem(spot + d, half) * 2 + core
        return copy(out.at[r], out.at[r], psend, precv, d, {"rows": peer})

    def aside(d):
        where = out.at[lax.rem(spot - d + half, half) * 2 + core]
        return copy(where, where, csend, crecv, d, {"rows": r + 1 - 2 * core})

    def first():
        for d in range(1, R):
            scatter(d).start()

    def second():
        total = w_ref[r]
        for d in range(1, R):
            scatter(d).wait()
            total = total + got[d]
        out[r, z] = total * (1.0 / count)
        for d in range(1, Z):
            along(d).start()

    def third():
        for d in range(1, Z):
            along(d).wait()
        for d in range(1, half):
            across(d).start()
        aside(0).start()

    def fourth():
        for d in range(1, half):
            across(d).wait()
            aside(d).start()

    def last():
        for d in range(half):
            aside(d).wait()

    return first, second, third, fourth, last


def invert_block(ref, dst):
    groups = TILE // 8
    a = [ref[8 * i : 8 * i + 8, :] for i in range(groups)]
    lane = lax.broadcasted_iota(jnp.int32, (8, TILE), 1)
    sub = lax.broadcasted_iota(jnp.int32, (8, TILE), 0)

    def across(v, j):
        return jnp.broadcast_to(v[:, j : j + 1], (8, TILE))

    def down(v, i):
        return jnp.broadcast_to(v[i : i + 1, :], (8, TILE))

    for g in range(groups):
        k = 8 * g
        c = [0.0 - across(a[g], k + j) for j in range(8)]
        far = [[across(a[i], k + j) if i != g else None for i in range(groups)] for j in range(8)]
        inside = jnp.logical_and(lane >= k, lane < k + 8)
        rows = jnp.where(inside, jnp.where(lane == sub + k, 1.0, 0.0), a[g])
        for s in range(0, 8, 2):
            p, q, r = down(c[s], s), down(c[s + 1], s), down(c[s + 1], s + 1)
            scale = 1.0 / (p * r - q * q)
            e0, e1, e2 = r * scale, -q * scale, p * scale
            pair = jnp.logical_and(sub >= s, sub < s + 2)
            l0 = jnp.where(pair, jnp.where(sub == s, 1.0, 0.0), c[s])
            l1 = jnp.where(pair, jnp.where(sub == s, 0.0, 1.0), c[s + 1])

            def step(v):
                v0, v1 = down(v, s), down(v, s + 1)
                w0, w1 = e0 * v0 + e1 * v1, e1 * v0 + e2 * v1
                return jnp.where(pair, 0.0, v) - (l0 * w0 + l1 * w1)

            rows = step(rows)
            for j in range(s + 2, 8):
                c[j] = step(c[j])
        w = [down(rows, i) for i in range(8)]
        for i in range(groups):
            if i == g:
                continue
            f = [far[j][i] * w[j] for j in range(8)]
            total = ((f[0] + f[1]) + (f[2] + f[3])) + ((f[4] + f[5]) + (f[6] + f[7]))
            a[i] = jnp.where(inside, 0.0, a[i]) - total
        a[g] = rows
    for i in range(groups):
        dst[8 * i : 8 * i + 8, :] = a[i]


def fused_kernel(
    R, Z, parts, count, x_ref, f_ref, t_hbm, coef_ref, low_ref, own_hbm,
    xs, t_ref, own, turned, acc, w, got, out, v, vgot, vout,
    gram, upper, lower, right, inverse, inner, send, recv, local, *rest
):
    phis, sems = rest[:parts], rest[parts:]
    r, z = lax.axis_index("rows"), lax.axis_index("rhs")
    size, panel = acc.shape
    chunk = x_ref.shape[1] // parts
    blocks = size // TILE
    load = pltpu.make_async_copy(t_hbm, t_ref, local.at[0])
    load.start()
    barrier = pltpu.get_barrier_semaphore()
    for d in range(1, R):
        pl.semaphore_signal(
            barrier, inc=1, device_id={"rows": lax.rem(r + d, R)}, device_id_type=MESH
        )
    for d in range(1, Z):
        pl.semaphore_signal(
            barrier, inc=1, device_id={"rhs": lax.rem(z + d, Z)}, device_id_type=MESH
        )
    pl.semaphore_wait(barrier, R + Z - 2)

    def moving(q, way):
        block, part = z - way * (q // parts), lax.rem(q, parts)
        if isinstance(q, int):
            source = x_ref.at[:, q * chunk : (q + 1) * chunk]
        else:
            source = xs.at[block, part]
        return pltpu.make_async_remote_copy(
            src_ref=source,
            dst_ref=xs.at[block, part],
            send_sem=send.at[(way + 1) // 2, q],
            recv_sem=recv.at[(way + 1) // 2, q],
            device_id={"rhs": z + way},
            device_id_type=MESH,
        )

    def arriving(q, way):
        block, part = z - way * (q // parts + 1), lax.rem(q, parts)
        return pltpu.make_async_remote_copy(
            src_ref=xs.at[block, part],
            dst_ref=xs.at[block, part],
            send_sem=send.at[(way + 1) // 2, q],
            recv_sem=recv.at[(way + 1) // 2, q],
            device_id={"rhs": z - way},
            device_id_type=MESH,
        )

    def inside(p):
        return jnp.logical_and(p >= 0, p < Z)

    for q in range(parts):
        for way in (1, -1):
            pl.when(inside(z + way))(lambda: moving(q, way).start())
    for part in range(parts):
        xs[z, part] = x_ref[:, part * chunk : (part + 1) * chunk]
    acc[...] = jnp.zeros_like(acc)
    near = jnp.minimum(z, Z - 1 - z)

    @pl.loop(0, Z)
    def _(d):
        for part in range(parts):
            q = (d - 1) * parts + part
            for way in (1, -1):

                @pl.when(jnp.logical_and(d > 0, inside(z - way * d)))
                def _():
                    arriving(q, way).wait_recv()
                    pl.when(inside(z + way))(lambda: moving(q + parts, way).start())

        step = (d + 1) // 2
        both = jnp.where(d % 2 == 1, z - step, z + step)
        single = jnp.where(z < Z - 1 - z, z + d - near, z - d + near)
        block = jnp.where(d <= 2 * near, both, single)
        for part, phi in enumerate(phis):
            phi[block] = features(xs[block, part], f_ref[...])
            mine = phi[block, pl.ds(pl.multiple_of(z * panel, panel), panel), :]
            turned[part] = mine.T
            acc[...] += jnp.dot(phi[block], turned[part], preferred_element_type=jnp.float32)

    @pl.loop(0, Z * parts)
    def _(q):
        for way in (1, -1):
            sent = jnp.logical_and(inside(z + way), inside(z - way * (q // parts)))
            pl.when(sent)(lambda: moving(q, way).wait_send())

    stages = [
        exchange(R, Z, count, w.at[c], got.at[c], out.at[c], [s.at[c] for s in sems[:8]])
        for c in range(blocks)
    ]
    rows = TILE // R
    for c in range(blocks):
        for i in range(R):
            at = c * TILE + i * rows
            w[c, i] = acc[at : at + rows, :]
        stages[c][0]()
    load.wait()
    acc[...] = jnp.zeros_like(acc)

    def cross(low, high):
        @pl.loop(low, high)
        def _(block):
            for part, phi in enumerate(phis):
                here = pl.multiple_of((block * parts + part) * chunk, chunk)
                acc[...] += jnp.dot(
                    phi[block], t_ref[pl.ds(here, chunk), :], preferred_element_type=jnp.float32
                )

    def keep(part):
        own[part] = phis[part][z].T
        pltpu.make_async_copy(own.at[part], own_hbm.at[part], local.at[1 + part]).start()

    def spread(source, dest, base, height):
        for i in range(R):
            for j in range(Z):
                top = base + i * height
                dest[top : top + height, j * panel : (j + 1) * panel] = source[i, j]

    cross(0, Z // 2)
    stages[0][1]()
    cross(Z // 2, Z)
    for c in range(1, blocks):
        stages[c][1]()
    stages[0][2]()
    high = size // R
    for i in range(R):
        v[i] = acc[i * high : (i + 1) * high, :]
    last = exchange(R, Z, count, v, vgot, vout, sems[8:])
    last[0]()
    for c in range(1, blocks):
        stages[c][2]()
    for part in range(parts):
        keep(part)
    stages[0][3]()
    for c in range(1, blocks):
        stages[c][3]()
    stages[0][4]()
    spread(out.at[0], gram, 0, rows)
    row = lax.broadcasted_iota(jnp.int32, (TILE, TILE), 0)
    col = lax.broadcasted_iota(jnp.int32, (TILE, TILE), 1)
    eye = jnp.where(row == col, jnp.float32(ridge), 0.0)
    dot = functools.partial(jnp.dot, precision=HIGHEST, preferred_element_type=jnp.float32)

    def at(i):
        return slice(i * TILE, (i + 1) * TILE)

    @pl.loop(0, blocks)
    def _(k):
        mine = pl.ds(pl.multiple_of(k * TILE, TILE), TILE)

        @pl.loop(0, k)
        def _(i):
            above = pl.ds(pl.multiple_of(i * TILE, TILE), TILE)
            left = upper[above, mine].T
            lower[mine, above] = left
            gram[mine, :] -= dot(left, gram[above, :])

        upper[mine, :] = gram[mine, :]
        inner[...] = gram[mine, mine] + eye
        invert_block(inner, inverse.at[k])
        gram[mine, :] = dot(inverse[k], upper[mine, :])
        for c in range(1, blocks):

            @pl.when(k == c - 1)
            def _():
                stages[c][4]()
                spread(out.at[c], gram, c * TILE, rows)

        for i, stage in enumerate(last[1:]):
            pl.when(k == min(i, blocks - 1))(stage)

    spread(vout, right, 0, high)
    for k in range(blocks):
        value = right[at(k), :]
        if k:
            value -= dot(lower[at(k), : k * TILE], right[: k * TILE, :])
        right[at(k), :] = dot(inverse[k], value)
    for k in reversed(range(blocks)):
        value = right[at(k), :]
        if k + 1 < blocks:
            value -= dot(gram[at(k), (k + 1) * TILE :], coef_ref[(k + 1) * TILE :, :])
        coef_ref[at(k), :] = value
        low_ref[at(k), :] = value.astype(jnp.bfloat16)
    for part in range(parts):
        pltpu.make_async_copy(own.at[part], own_hbm.at[part], local.at[1 + part]).wait()


def fused(x, freqs, targets):
    R, Z = lax.axis_size("rows"), lax.axis_size("rhs")
    depth, length = x.shape
    size = freqs.shape[0]
    panel = targets.shape[1]
    columns = Z * panel
    chunk = min(length, 512)
    parts = length // chunk
    blocks = size // TILE
    rows, high = TILE // R, size // R
    sems = pltpu.SemaphoreType.DMA
    f32, bf16 = jnp.float32, jnp.bfloat16
    return pl.pallas_call(
        functools.partial(fused_kernel, R, Z, parts, length * R * Z),
        out_shape=[
            jax.ShapeDtypeStruct((size, columns), f32),
            jax.ShapeDtypeStruct((size, columns), bf16),
            jax.ShapeDtypeStruct((parts, chunk, size), bf16),
        ],
        in_specs=[VMEM, VMEM, ANY],
        out_specs=[VMEM, VMEM, ANY],
        scratch_shapes=[
            pltpu.VMEM((Z, parts, depth, chunk), f32),
            pltpu.VMEM(targets.shape, targets.dtype),
            pltpu.VMEM((parts, chunk, size), bf16),
            pltpu.VMEM((parts, chunk, panel), bf16),
            pltpu.VMEM((size, panel), f32),
            pltpu.VMEM((blocks, R, rows, panel), f32),
            pltpu.VMEM((blocks, R, rows, panel), f32),
            pltpu.VMEM((blocks, R, Z, rows, panel), f32),
            pltpu.VMEM((R, high, panel), f32),
            pltpu.VMEM((R, high, panel), f32),
            pltpu.VMEM((R, Z, high, panel), f32),
            pltpu.VMEM((size, size), f32),
            pltpu.VMEM((size, size), f32),
            pltpu.VMEM((size, size), f32),
            pltpu.VMEM((size, columns), f32),
            pltpu.VMEM((blocks, TILE, TILE), f32),
            pltpu.VMEM((TILE, TILE), f32),
            sems((2, Z * parts)),
            sems((2, Z * parts)),
            sems((1 + parts,)),
        ]
        + [pltpu.VMEM((Z, size, chunk), bf16)] * parts
        + [sems((blocks, R))] * 2 + [sems((blocks, Z))] * 2 + [sems((blocks, R))] * 4
        + [sems((R,))] * 2 + [sems((Z,))] * 2 + [sems((R,))] * 4,
        compiler_params=pltpu.CompilerParams(collective_id=0, has_side_effects=True),
    )(x, freqs, targets)


def fit_kernel(own_ref, low_ref, coef_ref, coef_out, fitted_ref):
    coef_out[...] = coef_ref[...]
    fitted_ref[0] = jnp.dot(own_ref[0], low_ref[...], preferred_element_type=jnp.float32)


def fit(own, low, coef):
    parts, chunk, size = own.shape
    columns = low.shape[1]
    strip = size // parts
    return pl.pallas_call(
        fit_kernel,
        grid=(parts,),
        in_specs=[
            pl.BlockSpec((1, chunk, size), lambda i: (i, 0, 0)),
            pl.BlockSpec((size, columns), lambda i: (0, 0)),
            pl.BlockSpec((strip, columns), lambda i: (i, 0)),
        ],
        out_specs=[
            pl.BlockSpec((strip, columns), lambda i: (i, 0)),
            pl.BlockSpec((1, chunk, columns), lambda i: (i, 0, 0)),
        ],
        out_shape=[
            jax.ShapeDtypeStruct((size, columns), jnp.float32),
            jax.ShapeDtypeStruct((parts, chunk, columns), jnp.float32),
        ],
    )(own, low, coef)


def body(samples, freq_table, feature_seeds, phases, treatment_features):
    turn = jnp.float32(1.0 / (2.0 * math.pi))
    high, middle, low = split_low(freq_table[feature_seeds] * turn)
    shift = jnp.stack(split_low(phases * turn), axis=1)
    shift = jnp.pad(shift, ((0, 0), (0, high.shape[1] - shift.shape[1])))
    freqs = jnp.concatenate([high, middle, high, middle, low, high, shift], axis=1)
    coef, low_coef, own = fused(samples.T, freqs, treatment_features)
    coefficients, fitted = fit(own, low_coef, coef)
    return (coefficients, fitted.reshape(samples.shape[0], low_coef.shape[1]))


def solution(mesh):
    placed = (P(("rows", "rhs"), None), P(), P(), P(), P("rows", "rhs"))
    return jax.shard_map(
        body, mesh=mesh, in_specs=placed, out_specs=(P(), P(("rows", "rhs"), None)), check_vma=False
    )
```

time: 88.7 us -> 79 us (0.89)
  matrix products: 5.06 us -> 0 us
  Pallas kernels: 76.4 us -> 72.8 us
  local copies, waits for them, and re-layouts: 4.78 us -> 3.81 us
    dot_general x1 -> x0, matrix products: 5.06 us -> none  [body(): lax.dot_general(own, low_coef, (((1,), (0,)), ((), ())), preferred_elemen...]
    pallas_call x2, Pallas kernels: 76.4 us -> 72.8 us  [the longest x1 67.2 us: fused(): pl.pallas_call(functools.partial(fused_kernel, R, Z, parts, length * R *...]
    unnamed x4 -> x1, local copies, waits for them, and re-layouts: 2.52 us -> 1.55 us
where the time goes in v1:
time: 79 us; the launch traced here: 78.7 us
  Pallas kernels  72.8 us (92%)
  local copies, waits for them, and re-layouts  3.81 us (5%)
  other arithmetic  1.47 us (2%)
    pallas_call x1, Pallas kernels, fused(): pl.pallas_call(functools.partial(fused_kernel, R, Z, parts, length * R *...  67.2 us
    pallas_call x1, Pallas kernels, fit(): pl.pallas_call(fit_kernel, grid=(parts,), in_specs=[pl.BlockSpec((1, chun...  5.61 us

profile of v1, /device:TPU:0, one launch (start us, length us, event | category | flops | bytes accessed | tf_op | source)
XLA Modules:
  0.0 78.7 jit_solution(5879835749449702800)
XLA Ops:
  0.6 0.7 compare_select_fusion
  1.3 0.7 reduce-precision_convert_fusion.3
  2.1 0.2 copy.16
  2.3 1.5 %copy.14 = f32[4096,16]{1,0:T(8,128)S(1)} copy(f32[4096,16]{0,1:T(8,128)} %param.6) | data formatting | bytes 524288 | tf_op args[1]
  3.8 1.0 %gather_fusion = f32[512,16]{1,0:T(8,128)S(1)} fusion(f32[4096,16]{1,0:T(8,128)S(1)} %copy.14, s32[1024]{0:T(1024)S(1)} %pad_clamp_fusion), kind=kCustom, calls=%fused_computation | custom fusion | bytes 67584 | tf_op jit(solution)/shard_map/gather | solution.py:423
  4.9 0.1 fusion
  5.0 1.0 %concatenate.3.f_ref = bf16[512,112]{1,0:T(8,128)(2,1)} concatenate(bf16[512,16]{1,0:T(8,128)(2,1)S(1)} %get-tuple-element.14, bf16[512,16]{1,0:T(8,128)(2,1)S(1)} %get-tuple-element.13, bf16[512,16]{1,0:T(8,128)(2,1)S(1)} %get-tuple-element.14, bf16[512,16]{1,0:T(8,128)(2,1)S(1)} %get-tuple-element.13, bf16[512,16]{1,0:T(8,128)(2,1)S(1)} %get-tuple-element.12, ...), dimensions={1} | concatenate | bytes 229376 | tf_op jit(solution)/shard_map/concatenate | solution.py:426
  6.0 67.2 %shard_map.68 = (f32[512,512]{1,0:T(8,128)}, bf16[512,512]{1,0:T(8,128)(2,1)}, bf16[4,512,512]{2,1,0:T(8,128)(2,1)}) custom-call(f32[16,2048]{1,0:T(8,128)} %bitcast.2, bf16[512,112]{1,0:T(8,128)(2,1)} %concatenate.3.f_ref, bf16[8192,128]{1,0:T(8,128)(2,1)} %t_hbm.1), custom_call_target="tpu_custom_call" | custom-call | tf_op jit(solution)/shard_map/pallas_call | solution.py:355
  73.1 5.6 %shard_map.69 = (f32[512,512]{1,0:T(8,128)}, f32[4,512,512]{2,1,0:T(8,128)}) custom-call(bf16[4,512,512]{2,1,0:T(8,128)(2,1)} %get-tuple-element.7.own_ref, bf16[512,512]{1,0:T(8,128)(2,1)} %get-tuple-element.8.low_ref, f32[512,512]{1,0:T(8,128)} %get-tuple-element.9.coef_ref), custom_call_target="tpu_custom_call" | custom-call | tf_op jit(solution)/shard_map/pallas_call | solution.py:402
  (6 shorter events, 0.1 us)

commit v2 on v1

--- a/solution.py
+++ b/solution.py
@@ -13,23 +13,39 @@
 HIGHEST = lax.Precision.HIGHEST
 VMEM = pl.BlockSpec(memory_space=pltpu.VMEM)
 ANY = pl.BlockSpec(memory_space=pl.ANY)
+HBM = pl.BlockSpec(memory_space=pltpu.HBM)
 TILE = 128
 SIN_TERMS = [3.141592580044735, -5.1677068789267455, 2.550031377285281, -0.598045174146624, 0.07722012899537994]
 
 
-def split_low(x):
-    high = lax.reduce_precision(x, 8, 7)
-    rest = x - high
-    middle = lax.reduce_precision(rest, 8, 7)
-    low = rest - middle
-    return tuple(t.astype(jnp.bfloat16) for t in (high, middle, low))
+def split(x):
+    high = x.astype(jnp.bfloat16)
+    rest = x - high.astype(jnp.float32)
+    middle = rest.astype(jnp.bfloat16)
+    low = (rest - middle.astype(jnp.float32)).astype(jnp.bfloat16)
+    return high, middle, low
+
+
+def pick(table_ref, seed_ref, phase_ref):
+    turn = jnp.float32(1.0 / (2.0 * math.pi))
+    depth, length = table_ref.shape
+    size = seed_ref.shape[1]
+    tile = min(length, 512)
+    stack = jnp.concatenate(split(table_ref[...] * turn), axis=0)
+    row = lax.broadcasted_iota(jnp.int32, (tile, size), 0)
+    found = jnp.zeros((3 * depth, size), jnp.float32)
+    for k in range(0, length, tile):
+        chosen = jnp.where(row == seed_ref[...] - k, 1.0, 0.0).astype(jnp.bfloat16)
+        found += jnp.dot(stack[:, k : k + tile], chosen, preferred_element_type=jnp.float32)
+    high, middle, low = (found[i * depth : (i + 1) * depth] for i in range(3))
+    shift = [t.astype(jnp.float32) for t in split(phase_ref[...] * turn)]
+    shift = jnp.concatenate(shift + [jnp.zeros((depth - 3, size), jnp.float32)], axis=0)
+    full = jnp.concatenate([high, middle, high, middle, low, high, shift], axis=0)
+    return full.T.astype(jnp.bfloat16)
 
 
 def features(x, f):
-    high = x.astype(jnp.bfloat16)
-    left = x - high.astype(jnp.float32)
-    middle = left.astype(jnp.bfloat16)
-    low = (left - middle.astype(jnp.float32)).astype(jnp.bfloat16)
+    high, middle, low = split(x)
     ones = jnp.ones(x.shape, jnp.bfloat16)
     rows = jnp.concatenate([high, high, middle, middle, high, low, ones], axis=0)
     turns = jnp.dot(f, rows, preferred_element_type=jnp.float32)
@@ -106,64 +122,82 @@
     return first, second, third, fourth, last
 
 
-def invert_block(ref, dst):
-    groups = TILE // 8
-    a = [ref[8 * i : 8 * i + 8, :] for i in range(groups)]
-    lane = lax.broadcasted_iota(jnp.int32, (8, TILE), 1)
-    sub = lax.broadcasted_iota(jnp.int32, (8, TILE), 0)
+def sweep(a, base):
+    shape = a[0].shape
+    lane = lax.broadcasted_iota(jnp.int32, shape, 1)
+    sub = lax.broadcasted_iota(jnp.int32, shape, 0)
 
     def across(v, j):
-        return jnp.broadcast_to(v[:, j : j + 1], (8, TILE))
+        return jnp.broadcast_to(v[:, j : j + 1], shape)
 
     def down(v, i):
-        return jnp.broadcast_to(v[i : i + 1, :], (8, TILE))
-
-    for g in range(groups):
-        k = 8 * g
+        return jnp.broadcast_to(v[i : i + 1, :], shape)
+
+    for g in range(len(a)):
+        k = base + 8 * g
         c = [0.0 - across(a[g], k + j) for j in range(8)]
-        far = [[across(a[i], k + j) if i != g else None for i in range(groups)] for j in range(8)]
+        far = [[across(v, k + j) for j in range(8)] if i != g else None for i, v in enumerate(a)]
         inside = jnp.logical_and(lane >= k, lane < k + 8)
         rows = jnp.where(inside, jnp.where(lane == sub + k, 1.0, 0.0), a[g])
         for s in range(0, 8, 2):
             p, q, r = down(c[s], s), down(c[s + 1], s), down(c[s + 1], s + 1)
             scale = 1.0 / (p * r - q * q)
-            e0, e1, e2 = r * scale, -q * scale, p * scale
             pair = jnp.logical_and(sub >= s, sub < s + 2)
             l0 = jnp.where(pair, jnp.where(sub == s, 1.0, 0.0), c[s])
             l1 = jnp.where(pair, jnp.where(sub == s, 0.0, 1.0), c[s + 1])
 
             def step(v):
                 v0, v1 = down(v, s), down(v, s + 1)
-                w0, w1 = e0 * v0 + e1 * v1, e1 * v0 + e2 * v1
-                return jnp.where(pair, 0.0, v) - (l0 * w0 + l1 * w1)
+                u0, u1 = r * v0 - q * v1, p * v1 - q * v0
+                return jnp.where(pair, 0.0, v) - scale * (l0 * u0 + l1 * u1)
 
             rows = step(rows)
             for j in range(s + 2, 8):
                 c[j] = step(c[j])
         w = [down(rows, i) for i in range(8)]
-        for i in range(groups):
+        for i in range(len(a)):
             if i == g:
                 continue
-            f = [far[j][i] * w[j] for j in range(8)]
+            f = [far[i][j] * w[j] for j in range(8)]
             total = ((f[0] + f[1]) + (f[2] + f[3])) + ((f[4] + f[5]) + (f[6] + f[7]))
             a[i] = jnp.where(inside, 0.0, a[i]) - total
         a[g] = rows
+    return a
+
+
+def invert_block(ref, dst):
+    half = TILE // 2
+    groups = half // 8
+    dot = functools.partial(jnp.dot, precision=HIGHEST, preferred_element_type=jnp.float32)
+    left = lax.broadcasted_iota(jnp.int32, (half, TILE), 1) < half
+    top = sweep([ref[8 * i : 8 * i + 8, :] for i in range(groups)], 0)
     for i in range(groups):
-        dst[8 * i : 8 * i + 8, :] = a[i]
+        dst[8 * i : 8 * i + 8, :] = top[i]
+    lower = ref[half:, :]
+    lower = jnp.where(left, 0.0, lower) - dot(lower[:, :half], dst[:half, :])
+    low = sweep([lower[8 * i : 8 * i + 8, :] for i in range(groups)], half)
+    for i in range(groups):
+        dst[half + 8 * i : half + 8 * i + 8, :] = low[i]
+    upper = dst[:half, :]
+    dst[:half, :] = jnp.where(left, upper, 0.0) - dot(upper[:, half:], dst[half:, :])
 
 
 def fused_kernel(
-    R, Z, parts, count, x_ref, f_ref, t_hbm, coef_ref, low_ref, own_hbm,
-    xs, t_ref, own, turned, acc, w, got, out, v, vgot, vout,
+    R, Z, parts, count, x_hbm, table_hbm, seed_hbm, phase_hbm, t_hbm, coef_ref, low_ref, own,
+    xs, table_ref, seed_ref, phase_ref, t_ref, f_ref, turned, acc, w, got, out, v, vgot, vout,
     gram, upper, lower, right, inverse, inner, send, recv, local, *rest
 ):
     phis, sems = rest[:parts], rest[parts:]
     r, z = lax.axis_index("rows"), lax.axis_index("rhs")
     size, panel = acc.shape
-    chunk = x_ref.shape[1] // parts
+    chunk = x_hbm.shape[1] // parts
     blocks = size // TILE
-    load = pltpu.make_async_copy(t_hbm, t_ref, local.at[0])
-    load.start()
+    wanted = [(seed_hbm, seed_ref), (phase_hbm, phase_ref), (table_hbm, table_ref)]
+    wanted += [(x_hbm.at[:, i * chunk : (i + 1) * chunk], xs.at[z, i]) for i in range(parts)]
+    wanted += [(t_hbm, t_ref)]
+    loads = [pltpu.make_async_copy(*pair, local.at[i]) for i, pair in enumerate(wanted)]
+    for load in loads:
+        load.start()
     barrier = pltpu.get_barrier_semaphore()
     for d in range(1, R):
         pl.semaphore_signal(
@@ -178,7 +212,7 @@
     def moving(q, way):
         block, part = z - way * (q // parts), lax.rem(q, parts)
         if isinstance(q, int):
-            source = x_ref.at[:, q * chunk : (q + 1) * chunk]
+            source = x_hbm.at[:, q * chunk : (q + 1) * chunk]
         else:
             source = xs.at[block, part]
         return pltpu.make_async_remote_copy(
@@ -207,8 +241,9 @@
     for q in range(parts):
         for way in (1, -1):
             pl.when(inside(z + way))(lambda: moving(q, way).start())
-    for part in range(parts):
-        xs[z, part] = x_ref[:, part * chunk : (part + 1) * chunk]
+    for load in loads[:-1]:
+        load.wait()
+    f_ref[...] = pick(table_ref, seed_ref, phase_ref)
     acc[...] = jnp.zeros_like(acc)
     near = jnp.minimum(z, Z - 1 - z)
 
@@ -249,7 +284,7 @@
             at = c * TILE + i * rows
             w[c, i] = acc[at : at + rows, :]
         stages[c][0]()
-    load.wait()
+    loads[-1].wait()
     acc[...] = jnp.zeros_like(acc)
 
     def cross(low, high):
@@ -263,7 +298,6 @@
 
     def keep(part):
         own[part] = phis[part][z].T
-        pltpu.make_async_copy(own.at[part], own_hbm.at[part], local.at[1 + part]).start()
 
     def spread(source, dest, base, height):
         for i in range(R):
@@ -289,6 +323,7 @@
     stages[0][3]()
     for c in range(1, blocks):
         stages[c][3]()
+    last[1]()
     stages[0][4]()
     spread(out.at[0], gram, 0, rows)
     row = lax.broadcasted_iota(jnp.int32, (TILE, TILE), 0)
@@ -321,7 +356,7 @@
                 stages[c][4]()
                 spread(out.at[c], gram, c * TILE, rows)
 
-        for i, stage in enumerate(last[1:]):
+        for i, stage in enumerate(last[2:]):
             pl.when(k == min(i, blocks - 1))(stage)
 
     spread(vout, right, 0, high)
@@ -336,14 +371,12 @@
             value -= dot(gram[at(k), (k + 1) * TILE :], coef_ref[(k + 1) * TILE :, :])
         coef_ref[at(k), :] = value
         low_ref[at(k), :] = value.astype(jnp.bfloat16)
-    for part in range(parts):
-        pltpu.make_async_copy(own.at[part], own_hbm.at[part], local.at[1 + part]).wait()
-
-
-def fused(x, freqs, targets):
+
+
+def fused(x, table, seeds, phases, targets):
     R, Z = lax.axis_size("rows"), lax.axis_size("rhs")
     depth, length = x.shape
-    size = freqs.shape[0]
+    size = seeds.shape[1]
     panel = targets.shape[1]
     columns = Z * panel
     chunk = min(length, 512)
@@ -352,19 +385,23 @@
     rows, high = TILE // R, size // R
     sems = pltpu.SemaphoreType.DMA
     f32, bf16 = jnp.float32, jnp.bfloat16
+    place = lambda v: pltpu.with_memory_space_constraint(v, pltpu.HBM)
     return pl.pallas_call(
         functools.partial(fused_kernel, R, Z, parts, length * R * Z),
         out_shape=[
-            jax.ShapeDtypeStruct((size, columns), f32),
-            jax.ShapeDtypeStruct((size, columns), bf16),
-            jax.ShapeDtypeStruct((parts, chunk, size), bf16),
+            pltpu.VMEM((size, columns), f32),
+            pltpu.VMEM((size, columns), bf16),
+            pltpu.VMEM((parts, chunk, size), bf16),
         ],
-        in_specs=[VMEM, VMEM, ANY],
-        out_specs=[VMEM, VMEM, ANY],
+        in_specs=[HBM] * 5,
+        out_specs=[VMEM, VMEM, VMEM],
         scratch_shapes=[
             pltpu.VMEM((Z, parts, depth, chunk), f32),
+            pltpu.VMEM(table.shape, f32),
+            pltpu.VMEM(seeds.shape, jnp.int32),
+            pltpu.VMEM(phases.shape, f32),
             pltpu.VMEM(targets.shape, targets.dtype),
-            pltpu.VMEM((parts, chunk, size), bf16),
+            pltpu.VMEM((size, 7 * depth), bf16),
             pltpu.VMEM((parts, chunk, panel), bf16),
             pltpu.VMEM((size, panel), f32),
             pltpu.VMEM((blocks, R, rows, panel), f32),
@@ -381,50 +418,60 @@
             pltpu.VMEM((TILE, TILE), f32),
             sems((2, Z * parts)),
             sems((2, Z * parts)),
-            sems((1 + parts,)),
+            sems((4 + parts,)),
         ]
         + [pltpu.VMEM((Z, size, chunk), bf16)] * parts
         + [sems((blocks, R))] * 2 + [sems((blocks, Z))] * 2 + [sems((blocks, R))] * 4
         + [sems((R,))] * 2 + [sems((Z,))] * 2 + [sems((R,))] * 4,
-        compiler_params=pltpu.CompilerParams(collective_id=0, has_side_effects=True),
-    )(x, freqs, targets)
-
-
-def fit_kernel(own_ref, low_ref, coef_ref, coef_out, fitted_ref):
-    coef_out[...] = coef_ref[...]
-    fitted_ref[0] = jnp.dot(own_ref[0], low_ref[...], preferred_element_type=jnp.float32)
+        compiler_params=pltpu.CompilerParams(collective_id=0, has_side_effects=True, vmem_limit_bytes=40 << 20),
+    )(*map(place, (x, table, seeds, phases, targets)))
+
+
+def fit_kernel(own_ref, low_ref, coef_ref, coef_out, fitted_out, fitted, sems):
+    parts, chunk = own_ref.shape[:2]
+    copies = [pltpu.make_async_copy(coef_ref, coef_out, sems.at[0])]
+    copies[0].start()
+    half = chunk // 2
+    for part in range(parts):
+        for side in range(2):
+            rows = slice(side * half, (side + 1) * half)
+            fitted[part, rows, :] = jnp.dot(
+                own_ref[part, rows, :], low_ref[...], preferred_element_type=jnp.float32
+            )
+            i = 2 * part + side
+            copies.append(
+                pltpu.make_async_copy(
+                    fitted.at[part, rows], fitted_out.at[part, rows], sems.at[1 + i]
+                )
+            )
+            copies[-1].start()
+    for copy in copies:
+        copy.wait()
 
 
 def fit(own, low, coef):
     parts, chunk, size = own.shape
     columns = low.shape[1]
-    strip = size // parts
+    shape = (parts, chunk, columns)
     return pl.pallas_call(
         fit_kernel,
-        grid=(parts,),
-        in_specs=[
-            pl.BlockSpec((1, chunk, size), lambda i: (i, 0, 0)),
-            pl.BlockSpec((size, columns), lambda i: (0, 0)),
-            pl.BlockSpec((strip, columns), lambda i: (i, 0)),
-        ],
-        out_specs=[
-            pl.BlockSpec((strip, columns), lambda i: (i, 0)),
-            pl.BlockSpec((1, chunk, columns), lambda i: (i, 0, 0)),
-        ],
+        in_specs=[VMEM, VMEM, VMEM],
+        out_specs=[ANY, ANY],
         out_shape=[
             jax.ShapeDtypeStruct((size, columns), jnp.float32),
-            jax.ShapeDtypeStruct((parts, chunk, columns), jnp.float32),
+            jax.ShapeDtypeStruct(shape, jnp.float32),
         ],
+        scratch_shapes=[
+            pltpu.VMEM(shape, jnp.float32),
+            pltpu.SemaphoreType.DMA((1 + 2 * parts,)),
+        ],
+        compiler_params=pltpu.CompilerParams(vmem_limit_bytes=16 << 20),
     )(own, low, coef)
 
 
 def body(samples, freq_table, feature_seeds, phases, treatment_features):
-    turn = jnp.float32(1.0 / (2.0 * math.pi))
-    high, middle, low = split_low(freq_table[feature_seeds] * turn)
-    shift = jnp.stack(split_low(phases * turn), axis=1)
-    shift = jnp.pad(shift, ((0, 0), (0, high.shape[1] - shift.shape[1])))
-    freqs = jnp.concatenate([high, middle, high, middle, low, high, shift], axis=1)
-    coef, low_coef, own = fused(samples.T, freqs, treatment_features)
+    seeds, shifts = feature_seeds.reshape(1, -1), phases.reshape(1, -1)
+    coef, low_coef, own = fused(samples.T, freq_table.T, seeds, shifts, treatment_features)
     coefficients, fitted = fit(own, low_coef, coef)
     return (coefficients, fitted.reshape(samples.shape[0], low_coef.shape[1]))
 

time: 79 us -> 65.9 us (0.83)
  Pallas kernels: 72.8 us -> 65 us
  local copies, waits for them, and re-layouts: 3.81 us -> 0 us
  other arithmetic: 1.47 us -> 0 us
    pallas_call x1, Pallas kernels: 67.2 us -> 62.6 us  [fused(): pl.pallas_call(functools.partial(fused_kernel, R, Z, parts, length * R *...]
    pallas_call x1, Pallas kernels: 5.61 us -> 2.43 us  [fit(): pl.pallas_call(fit_kernel, in_specs=[VMEM, VMEM, VMEM], out_specs=[ANY, A...]
    unnamed x1 -> x0, local copies, waits for them, and re-layouts: 1.55 us -> none
    gather x1 -> x0, local copies, waits for them, and re-layouts: 1.04 us -> none  [body(): high, middle, low = split_low(freq_table[feature_seeds] * turn)]
    concatenate x1 -> x0, local copies, waits for them, and re-layouts: 1 us -> none  [body(): jnp.concatenate([high, middle, high, middle, low, high, shift], axis=1)]
where the time goes in v2:
time: 65.9 us; the launch traced here: 65.8 us
  Pallas kernels  65 us (99%)
  between operations  0.8 us (1%)
    pallas_call x1, Pallas kernels, fused(): pl.pallas_call(functools.partial(fused_kernel, R, Z, parts, length * R *...  62.6 us
    pallas_call x1, Pallas kernels, fit(): pl.pallas_call(fit_kernel, in_specs=[VMEM, VMEM, VMEM], out_specs=[ANY, A...  2.43 us

profile of v2, /device:TPU:0, one launch (start us, length us, event | category | flops | bytes accessed | tf_op | source)
XLA Modules:
  0.0 65.8 jit_solution(1503706837893121384)
XLA Ops:
  0.6 62.6 %shard_map.68 = (f32[512,512]{1,0:T(8,128)S(1)}, bf16[512,512]{1,0:T(8,128)(2,1)S(1)}, bf16[4,512,512]{2,1,0:T(8,128)(2,1)S(1)}) custom-call(f32[16,2048]{1,0:T(8,128)} %bitcast.6, f32[16,4096]{1,0:T(8,128)} %bitcast.5, s32[1,512]{1,0:T(1,128)} %bitcast.7, f32[1,512]{1,0:T(1,128)} %bitcast.8, bf16[8192,128]{1,0:T(8,128)(2,1)} %t_hbm.1), custom_call_target="tpu_custom_call" | custom-call | tf_op jit(solution)/shard_map/pallas_call | solution.py:389
  63.2 2.4 %shard_map.69 = (f32[512,512]{1,0:T(8,128)}, f32[4,512,512]{2,1,0:T(8,128)}) custom-call(bf16[4,512,512]{2,1,0:T(8,128)(2,1)S(1)} %get-tuple-element.7.own_ref, bf16[512,512]{1,0:T(8,128)(2,1)S(1)} %get-tuple-element.8.low_ref, f32[512,512]{1,0:T(8,128)S(1)} %get-tuple-element.9.coef_ref), custom_call_target="tpu_custom_call" | custom-call | tf_op jit(solution)/shard_map/pallas_call | solution.py:456

commit v3 on v2

--- a/solution.py
+++ b/solution.py
@@ -59,10 +59,13 @@
     return (math.sqrt(2.0) - s * s).astype(jnp.bfloat16)
 
 
-def exchange(R, Z, count, w_ref, got, out, sems):
+def exchange(R, Z, low, count, w_ref, got, out, sems):
     send, recv, zsend, zrecv, psend, precv, csend, crecv = sems
     r, z = lax.axis_index("rows"), lax.axis_index("rhs")
     core, spot, half = lax.rem(r, 2), r // 2, R // 2
+
+    def holds(column):
+        return (lambda f: f()) if low == 0 else pl.when(column >= low)
 
     def copy(src, dst, out_sem, in_sem, d, peer):
         return pltpu.make_async_remote_copy(
@@ -84,28 +87,33 @@
 
     def across(d):
         peer = lax.rem(spot + d, half) * 2 + core
-        return copy(out.at[r], out.at[r], psend, precv, d, {"rows": peer})
+        where = out.at[r, low:]
+        return copy(where, where, psend, precv, d, {"rows": peer})
 
     def aside(d):
-        where = out.at[lax.rem(spot - d + half, half) * 2 + core]
+        where = out.at[lax.rem(spot - d + half, half) * 2 + core, low:]
         return copy(where, where, csend, crecv, d, {"rows": r + 1 - 2 * core})
 
     def first():
-        for d in range(1, R):
-            scatter(d).start()
+        @holds(z)
+        def _():
+            for d in range(1, R):
+                scatter(d).start()
 
     def second():
-        total = w_ref[r]
-        for d in range(1, R):
-            scatter(d).wait()
-            total = total + got[d]
-        out[r, z] = total * (1.0 / count)
-        for d in range(1, Z):
-            along(d).start()
+        @holds(z)
+        def _():
+            total = w_ref[r]
+            for d in range(1, R):
+                scatter(d).wait()
+                total = total + got[d]
+            out[r, z] = total * (1.0 / count)
+            for d in range(1, Z):
+                along(d).start()
 
     def third():
         for d in range(1, Z):
-            along(d).wait()
+            holds(lax.rem(z - d + Z, Z))(along(d).wait_recv)
         for d in range(1, half):
             across(d).start()
         aside(0).start()
@@ -118,6 +126,11 @@
     def last():
         for d in range(half):
             aside(d).wait()
+
+        @holds(z)
+        def _():
+            for d in range(1, Z):
+                along(d).wait_send()
 
     return first, second, third, fourth, last
 
@@ -189,7 +202,7 @@
 ):
     phis, sems = rest[:parts], rest[parts:]
     r, z = lax.axis_index("rows"), lax.axis_index("rhs")
-    size, panel = acc.shape
+    size, panel = acc.shape[0], t_ref.shape[1]
     chunk = x_hbm.shape[1] // parts
     blocks = size // TILE
     wanted = [(seed_hbm, seed_ref), (phase_hbm, phase_ref), (table_hbm, table_ref)]
@@ -241,7 +254,7 @@
     for q in range(parts):
         for way in (1, -1):
             pl.when(inside(z + way))(lambda: moving(q, way).start())
-    for load in loads[:-1]:
+    for load in loads:
         load.wait()
     f_ref[...] = pick(table_ref, seed_ref, phase_ref)
     acc[...] = jnp.zeros_like(acc)
@@ -265,7 +278,9 @@
         for part, phi in enumerate(phis):
             phi[block] = features(xs[block, part], f_ref[...])
             mine = phi[block, pl.ds(pl.multiple_of(z * panel, panel), panel), :]
-            turned[part] = mine.T
+            turned[part, :, :panel] = mine.T
+            here = pl.multiple_of((block * parts + part) * chunk, chunk)
+            turned[part, :, panel:] = t_ref[pl.ds(here, chunk), :]
             acc[...] += jnp.dot(phi[block], turned[part], preferred_element_type=jnp.float32)
 
     @pl.loop(0, Z * parts)
@@ -275,55 +290,42 @@
             pl.when(sent)(lambda: moving(q, way).wait_send())
 
     stages = [
-        exchange(R, Z, count, w.at[c], got.at[c], out.at[c], [s.at[c] for s in sems[:8]])
+        exchange(
+            R, Z, c * TILE // panel, count, w.at[c], got.at[c], out.at[c],
+            [s.at[c] for s in sems[:8]],
+        )
         for c in range(blocks)
     ]
     rows = TILE // R
     for c in range(blocks):
         for i in range(R):
             at = c * TILE + i * rows
-            w[c, i] = acc[at : at + rows, :]
+            w[c, i] = acc[at : at + rows, :panel]
         stages[c][0]()
-    loads[-1].wait()
-    acc[...] = jnp.zeros_like(acc)
-
-    def cross(low, high):
-        @pl.loop(low, high)
-        def _(block):
-            for part, phi in enumerate(phis):
-                here = pl.multiple_of((block * parts + part) * chunk, chunk)
-                acc[...] += jnp.dot(
-                    phi[block], t_ref[pl.ds(here, chunk), :], preferred_element_type=jnp.float32
-                )
+    high = size // R
+    for i in range(R):
+        v[i] = acc[i * high : (i + 1) * high, panel:]
+    last = exchange(R, Z, 0, count, v, vgot, vout, sems[8:])
+    last[0]()
 
     def keep(part):
         own[part] = phis[part][z].T
 
-    def spread(source, dest, base, height):
+    def spread(source, dest, base, height, first=0):
         for i in range(R):
-            for j in range(Z):
+            for j in range(first, Z):
                 top = base + i * height
                 dest[top : top + height, j * panel : (j + 1) * panel] = source[i, j]
 
-    cross(0, Z // 2)
-    stages[0][1]()
-    cross(Z // 2, Z)
-    for c in range(1, blocks):
-        stages[c][1]()
-    stages[0][2]()
-    high = size // R
-    for i in range(R):
-        v[i] = acc[i * high : (i + 1) * high, :]
-    last = exchange(R, Z, count, v, vgot, vout, sems[8:])
-    last[0]()
-    for c in range(1, blocks):
-        stages[c][2]()
+    for step in (1, 2):
+        for c in range(blocks):
+            stages[c][step]()
     for part in range(parts):
         keep(part)
     stages[0][3]()
+    last[1]()
     for c in range(1, blocks):
         stages[c][3]()
-    last[1]()
     stages[0][4]()
     spread(out.at[0], gram, 0, rows)
     row = lax.broadcasted_iota(jnp.int32, (TILE, TILE), 0)
@@ -354,9 +356,9 @@
             @pl.when(k == c - 1)
             def _():
                 stages[c][4]()
-                spread(out.at[c], gram, c * TILE, rows)
-
-        for i, stage in enumerate(last[2:]):
+                spread(out.at[c], gram, c * TILE, rows, c * TILE // panel)
+
+        for i, stage in ((0, last[2]), (2, last[3]), (3, last[4])):
             pl.when(k == min(i, blocks - 1))(stage)
 
     spread(vout, right, 0, high)
@@ -402,8 +404,8 @@
             pltpu.VMEM(phases.shape, f32),
             pltpu.VMEM(targets.shape, targets.dtype),
             pltpu.VMEM((size, 7 * depth), bf16),
-            pltpu.VMEM((parts, chunk, panel), bf16),
-            pltpu.VMEM((size, panel), f32),
+            pltpu.VMEM((parts, chunk, 2 * panel), bf16),
+            pltpu.VMEM((size, 2 * panel), f32),
             pltpu.VMEM((blocks, R, rows, panel), f32),
             pltpu.VMEM((blocks, R, rows, panel), f32),
             pltpu.VMEM((blocks, R, Z, rows, panel), f32),

time: 65.9 us -> 59.1 us (0.90)
  Pallas kernels: 65 us -> 58.1 us
    pallas_call x1, Pallas kernels: 62.6 us -> 55.7 us  [fused(): pl.pallas_call(functools.partial(fused_kernel, R, Z, parts, length * R *...]
where the time goes in v3:
time: 59.1 us; the launch traced here: 58.9 us
  Pallas kernels  58.1 us (98%)
  between operations  0.8 us (1%)
    pallas_call x1, Pallas kernels, fused(): pl.pallas_call(functools.partial(fused_kernel, R, Z, parts, length * R *...  55.7 us
    pallas_call x1, Pallas kernels, fit(): pl.pallas_call(fit_kernel, in_specs=[VMEM, VMEM, VMEM], out_specs=[ANY, A...  2.43 us

profile of v3, /device:TPU:0, one launch (start us, length us, event | category | flops | bytes accessed | tf_op | source)
XLA Modules:
  0.0 58.9 jit_solution(13867890598525819157)
XLA Ops:
  0.6 55.7 %shard_map.68 = (f32[512,512]{1,0:T(8,128)S(1)}, bf16[512,512]{1,0:T(8,128)(2,1)S(1)}, bf16[4,512,512]{2,1,0:T(8,128)(2,1)S(1)}) custom-call(f32[16,2048]{1,0:T(8,128)} %bitcast.6, f32[16,4096]{1,0:T(8,128)} %bitcast.5, s32[1,512]{1,0:T(1,128)} %bitcast.7, f32[1,512]{1,0:T(1,128)} %bitcast.8, bf16[8192,128]{1,0:T(8,128)(2,1)} %t_hbm.1), custom_call_target="tpu_custom_call" | custom-call | tf_op jit(solution)/shard_map/pallas_call | solution.py:391
  56.4 2.4 %shard_map.69 = (f32[512,512]{1,0:T(8,128)}, f32[4,512,512]{2,1,0:T(8,128)}) custom-call(bf16[4,512,512]{2,1,0:T(8,128)(2,1)S(1)} %get-tuple-element.7.own_ref, bf16[512,512]{1,0:T(8,128)(2,1)S(1)} %get-tuple-element.8.low_ref, f32[512,512]{1,0:T(8,128)S(1)} %get-tuple-element.9.coef_ref), custom_call_target="tpu_custom_call" | custom-call | tf_op jit(solution)/shard_map/pallas_call | solution.py:458

commit v4 on v3

--- a/solution.py
+++ b/solution.py
@@ -24,6 +24,16 @@
     middle = rest.astype(jnp.bfloat16)
     low = (rest - middle.astype(jnp.float32)).astype(jnp.bfloat16)
     return high, middle, low
+
+
+def exact(a, b):
+    ah, am, al = split(a)
+    bh, bm, bl = split(b)
+    return jnp.dot(
+        jnp.concatenate([am, al, am, ah, ah, ah], axis=1),
+        jnp.concatenate([bm, bh, bh, bl, bm, bh], axis=0),
+        preferred_element_type=jnp.float32,
+    )
 
 
 def pick(table_ref, seed_ref, phase_ref):
@@ -254,11 +264,24 @@
     for q in range(parts):
         for way in (1, -1):
             pl.when(inside(z + way))(lambda: moving(q, way).start())
-    for load in loads:
+    for load in loads[:-1]:
         load.wait()
     f_ref[...] = pick(table_ref, seed_ref, phase_ref)
+    loads[-1].wait()
     acc[...] = jnp.zeros_like(acc)
     near = jnp.minimum(z, Z - 1 - z)
+
+    def visit(d):
+        step = (d + 1) // 2
+        both = jnp.where(d % 2 == 1, z - step, z + step)
+        single = jnp.where(z < Z - 1 - z, z + d - near, z - d + near)
+        return jnp.where(d <= 2 * near, both, single)
+
+    def gather(part, block):
+        acc[...] += jnp.dot(phis[part][block], turned[part], preferred_element_type=jnp.float32)
+
+    phis[-1][z] = jnp.zeros(phis[-1].shape[1:], jnp.bfloat16)
+    turned[parts - 1] = jnp.zeros(turned.shape[1:], jnp.bfloat16)
 
     @pl.loop(0, Z)
     def _(d):
@@ -271,24 +294,18 @@
                     arriving(q, way).wait_recv()
                     pl.when(inside(z + way))(lambda: moving(q + parts, way).start())
 
-        step = (d + 1) // 2
-        both = jnp.where(d % 2 == 1, z - step, z + step)
-        single = jnp.where(z < Z - 1 - z, z + d - near, z - d + near)
-        block = jnp.where(d <= 2 * near, both, single)
+        block = visit(d)
+        gather(parts - 1, visit(jnp.maximum(d - 1, 0)))
         for part, phi in enumerate(phis):
             phi[block] = features(xs[block, part], f_ref[...])
             mine = phi[block, pl.ds(pl.multiple_of(z * panel, panel), panel), :]
             turned[part, :, :panel] = mine.T
             here = pl.multiple_of((block * parts + part) * chunk, chunk)
             turned[part, :, panel:] = t_ref[pl.ds(here, chunk), :]
-            acc[...] += jnp.dot(phi[block], turned[part], preferred_element_type=jnp.float32)
-
-    @pl.loop(0, Z * parts)
-    def _(q):
-        for way in (1, -1):
-            sent = jnp.logical_and(inside(z + way), inside(z - way * (q // parts)))
-            pl.when(sent)(lambda: moving(q, way).wait_send())
-
+            if part + 1 < parts:
+                gather(part, block)
+
+    gather(parts - 1, visit(Z - 1))
     stages = [
         exchange(
             R, Z, c * TILE // panel, count, w.at[c], got.at[c], out.at[c],
@@ -308,6 +325,12 @@
     last = exchange(R, Z, 0, count, v, vgot, vout, sems[8:])
     last[0]()
 
+    @pl.loop(0, Z * parts)
+    def _(q):
+        for way in (1, -1):
+            sent = jnp.logical_and(inside(z + way), inside(z - way * (q // parts)))
+            pl.when(sent)(lambda: moving(q, way).wait_send())
+
     def keep(part):
         own[part] = phis[part][z].T
 
@@ -331,7 +354,7 @@
     row = lax.broadcasted_iota(jnp.int32, (TILE, TILE), 0)
     col = lax.broadcasted_iota(jnp.int32, (TILE, TILE), 1)
     eye = jnp.where(row == col, jnp.float32(ridge), 0.0)
-    dot = functools.partial(jnp.dot, precision=HIGHEST, preferred_element_type=jnp.float32)
+    dot = exact
 
     def at(i):
         return slice(i * TILE, (i + 1) * TILE)

time: 59.1 us -> 56.7 us (0.959)
  Pallas kernels: 58.1 us -> 55.9 us
    pallas_call x1, Pallas kernels: 55.7 us -> 53.4 us  [fused(): pl.pallas_call(functools.partial(fused_kernel, R, Z, parts, length * R *...]
where the time goes in v4:
time: 56.7 us; the launch traced here: 56.5 us
  Pallas kernels  55.9 us (99%)
  between operations  0.64 us (1%)
    pallas_call x1, Pallas kernels, fused(): pl.pallas_call(functools.partial(fused_kernel, R, Z, parts, length * R *...  53.4 us
    pallas_call x1, Pallas kernels, fit(): pl.pallas_call(fit_kernel, in_specs=[VMEM, VMEM, VMEM], out_specs=[ANY, A...  2.43 us

profile of v4, /device:TPU:0, one launch (start us, length us, event | category | flops | bytes accessed | tf_op | source)
XLA Modules:
  0.0 56.5 jit_solution(10675736370753374737)
XLA Ops:
  0.6 53.4 %shard_map.68 = (f32[512,512]{1,0:T(8,128)S(1)}, bf16[512,512]{1,0:T(8,128)(2,1)S(1)}, bf16[4,512,512]{2,1,0:T(8,128)(2,1)S(1)}) custom-call(f32[16,2048]{1,0:T(8,128)} %bitcast.6, f32[16,4096]{1,0:T(8,128)} %bitcast.5, s32[1,512]{1,0:T(1,128)} %bitcast.7, f32[1,512]{1,0:T(1,128)} %bitcast.8, bf16[8192,128]{1,0:T(8,128)(2,1)} %t_hbm.1), custom_call_target="tpu_custom_call" | custom-call | tf_op jit(solution)/shard_map/pallas_call | solution.py:414
  54.1 2.4 %shard_map.69 = (f32[512,512]{1,0:T(8,128)}, f32[4,512,512]{2,1,0:T(8,128)}) custom-call(bf16[4,512,512]{2,1,0:T(8,128)(2,1)S(1)} %get-tuple-element.7.own_ref, bf16[512,512]{1,0:T(8,128)(2,1)S(1)} %get-tuple-element.8.low_ref, f32[512,512]{1,0:T(8,128)S(1)} %get-tuple-element.9.coef_ref), custom_call_target="tpu_custom_call" | custom-call | tf_op jit(solution)/shard_map/pallas_call | solution.py:481

commit v5 on v4

--- a/solution.py
+++ b/solution.py
@@ -159,7 +159,7 @@
     for g in range(len(a)):
         k = base + 8 * g
         c = [0.0 - across(a[g], k + j) for j in range(8)]
-        far = [[across(v, k + j) for j in range(8)] if i != g else None for i, v in enumerate(a)]
+        far = [[across(v, k + j) if i != g else None for i, v in enumerate(a)] for j in range(8)]
         inside = jnp.logical_and(lane >= k, lane < k + 8)
         rows = jnp.where(inside, jnp.where(lane == sub + k, 1.0, 0.0), a[g])
         for s in range(0, 8, 2):
@@ -181,7 +181,7 @@
         for i in range(len(a)):
             if i == g:
                 continue
-            f = [far[i][j] * w[j] for j in range(8)]
+            f = [far[j][i] * w[j] for j in range(8)]
             total = ((f[0] + f[1]) + (f[2] + f[3])) + ((f[4] + f[5]) + (f[6] + f[7]))
             a[i] = jnp.where(inside, 0.0, a[i]) - total
         a[g] = rows
@@ -359,30 +359,24 @@
     def at(i):
         return slice(i * TILE, (i + 1) * TILE)
 
-    @pl.loop(0, blocks)
-    def _(k):
-        mine = pl.ds(pl.multiple_of(k * TILE, TILE), TILE)
-
-        @pl.loop(0, k)
-        def _(i):
-            above = pl.ds(pl.multiple_of(i * TILE, TILE), TILE)
-            left = upper[above, mine].T
-            lower[mine, above] = left
-            gram[mine, :] -= dot(left, gram[above, :])
-
-        upper[mine, :] = gram[mine, :]
-        inner[...] = gram[mine, mine] + eye
+    for k in range(blocks):
+        ahead = slice(k * TILE, size)
+        value = gram[at(k), ahead]
+        if k:
+            left = upper[: k * TILE, at(k)].T
+            lower[at(k), : k * TILE] = left
+            value -= dot(left, gram[: k * TILE, ahead])
+        upper[at(k), ahead] = value
+        inner[...] = value[:, :TILE] + eye
         invert_block(inner, inverse.at[k])
-        gram[mine, :] = dot(inverse[k], upper[mine, :])
-        for c in range(1, blocks):
-
-            @pl.when(k == c - 1)
-            def _():
-                stages[c][4]()
-                spread(out.at[c], gram, c * TILE, rows, c * TILE // panel)
-
+        if k + 1 < blocks:
+            after = slice((k + 1) * TILE, size)
+            gram[at(k), after] = dot(inverse[k], upper[at(k), after])
+            stages[k + 1][4]()
+            spread(out.at[k + 1], gram, (k + 1) * TILE, rows, (k + 1) * TILE // panel)
         for i, stage in ((0, last[2]), (2, last[3]), (3, last[4])):
-            pl.when(k == min(i, blocks - 1))(stage)
+            if k == min(i, blocks - 1):
+                stage()
 
     spread(vout, right, 0, high)
     for k in range(blocks):

time: 56.7 us -> 56.1 us (0.989)
  Pallas kernels: 55.9 us -> 55.1 us
    pallas_call x1, Pallas kernels: 53.4 us -> 52.7 us  [fused(): pl.pallas_call(functools.partial(fused_kernel, R, Z, parts, length * R *...]
where the time goes in v5:
time: 56.1 us; the launch traced here: 55.9 us
  Pallas kernels  55.1 us (98%)
  between operations  0.8 us (1%)
    pallas_call x1, Pallas kernels, fused(): pl.pallas_call(functools.partial(fused_kernel, R, Z, parts, length * R *...  52.7 us
    pallas_call x1, Pallas kernels, fit(): pl.pallas_call(fit_kernel, in_specs=[VMEM, VMEM, VMEM], out_specs=[ANY, A...  2.43 us

profile of v5, /device:TPU:0, one launch (start us, length us, event | category | flops | bytes accessed | tf_op | source)
XLA Modules:
  0.0 55.9 jit_solution(6649247348007845964)
XLA Ops:
  0.6 52.7 %shard_map.68 = (f32[512,512]{1,0:T(8,128)S(1)}, bf16[512,512]{1,0:T(8,128)(2,1)S(1)}, bf16[4,512,512]{2,1,0:T(8,128)(2,1)S(1)}) custom-call(f32[16,2048]{1,0:T(8,128)} %bitcast.6, f32[16,4096]{1,0:T(8,128)} %bitcast.5, s32[1,512]{1,0:T(1,128)} %bitcast.7, f32[1,512]{1,0:T(1,128)} %bitcast.8, bf16[8192,128]{1,0:T(8,128)(2,1)} %t_hbm.1), custom_call_target="tpu_custom_call" | custom-call | tf_op jit(solution)/shard_map/pallas_call | solution.py:408
  53.4 2.4 %shard_map.69 = (f32[512,512]{1,0:T(8,128)}, f32[4,512,512]{2,1,0:T(8,128)}) custom-call(bf16[4,512,512]{2,1,0:T(8,128)(2,1)S(1)} %get-tuple-element.7.own_ref, bf16[512,512]{1,0:T(8,128)(2,1)S(1)} %get-tuple-element.8.low_ref, f32[512,512]{1,0:T(8,128)S(1)} %get-tuple-element.9.coef_ref), custom_call_target="tpu_custom_call" | custom-call | tf_op jit(solution)/shard_map/pallas_call | solution.py:475
